TPU v7x, 32 devices: a whole 2x2x4 slice. The times are simulated.
32 devices in a mesh: aux: 4 (over y, x), blk: 8 (over z, core).
Axes of the slice: x: 2, y: 2, z: 4, core: 2. Of those that a mesh axis runs over, the one named last changes fastest.
Arguments:
- integrals: bfloat16 [2048, 64, 1024], P(('aux', 'blk')), may hold values from -0.5 to 0.5
- metric: bfloat16 [2048, 512], P('aux'), may hold values from -1 to 2
- pair_list: int32 [15, 2], replicated, may hold values from 0 to 7, as said below
- aux_mask: int32 [16, 8], P('aux'), may hold values 0 or 1
Outputs:
- band_rows: float32 [8, 128, 640], P('blk', 'aux')
Inputs may be any that keep to these rules, and one draw needn't show every extreme that they name: `pair_list`: every pair (r, r) appears once; the other rows are distinct pairs (r, r + 1) or (r, r + 2) with both blocks below 8; 7 such rows.
All inputs are finite; a program needn't handle non-finite values. No bound on the sum of `aux_mask` on one device may be relied on, other than what follows from the above.
Results may differ from a plain program's by a relative error of at most 0.0015.
Values may be sent and summed in bfloat16 or wider, within the bound.
A program may use at most 128 MiB of HBM per device.

v0:
```python
import jax
import jax.numpy as jnp
from jax import lax
from jax.sharding import PartitionSpec as P

BS = 128
QB = 128
SPAN = 3


def from_behind(array, axis, by):
    peers = lax.axis_size(axis)
    pairs = [(i, i + by) for i in range(peers) if 0 <= i + by < peers]
    return lax.ppermute(array, axis, pairs)


def fit_block(metric, slab_piece, mask_rows):
    fitted = jnp.einsum("pq,qjn->pjn", metric, slab_piece, preferred_element_type=jnp.float32)
    return (fitted * mask_rows[:, None, None]).astype(jnp.bfloat16)


def local(integrals, metric, pair_list, aux_mask):
    block_count = aux_mask.shape[1]
    position = lax.axis_index("blk")
    block_ids = jnp.arange(block_count, dtype=jnp.int32)
    offsets = jnp.arange(SPAN, dtype=jnp.int32)
    col_gap = pair_list[:, 1] - pair_list[:, 0]
    hits = (pair_list[:, 0][:, None] == position) & (col_gap[:, None] == offsets[None, :])
    listed = jnp.sum(hits.astype(jnp.int32), axis=0)
    one_hot = (block_ids == position).astype(jnp.int32)
    column = jnp.sum(aux_mask * one_hot[None, :], axis=1)
    own_mask = jnp.repeat(column, QB).astype(jnp.float32)
    own_block = fit_block(
        metric, lax.all_to_all(integrals, "blk", split_axis=2, concat_axis=0, tiled=True), own_mask
    )
    partners = [own_block]
    current = own_block
    for turn_index in range(SPAN - 1):
        current = from_behind(current, "blk", -1)
        partners.append(current)
    flat_own = partners[0].reshape(-1, BS)

    def make_tile(partner):
        return lax.dot_general(
            flat_own,
            partner.reshape(-1, BS),
            (((0,), (0,)), ((), ())),
            preferred_element_type=jnp.float32,
        )

    tile_list = [
        make_tile(partners[offset]) * listed[offset].astype(jnp.float32) for offset in range(SPAN)
    ]
    upper_tiles = jnp.stack(tile_list)
    mirror_tiles = jnp.stack([jnp.transpose(tile_list[offset]) for offset in range(1, SPAN)])
    lower_tiles = []
    moving = mirror_tiles
    for turn_index in range(SPAN - 1):
        moving = from_behind(moving.astype(jnp.bfloat16), "blk", 1).astype(moving.dtype)
        lower_tiles.append(moving[0])
        moving = moving[1:]
    whole_band = jnp.concatenate(
        [jnp.stack([lower_tiles[SPAN - 2 - slot] for slot in range(SPAN - 1)]), upper_tiles], axis=0
    )
    band_parts = lax.psum_scatter(whole_band, "aux", scatter_dimension=1, tiled=True)
    pieces = [band_parts[slot] for slot in range(2 * SPAN - 1)]
    band_rows = jnp.concatenate(pieces, axis=1)
    return band_rows[None]


def solution(mesh):
    return jax.shard_map(
        local,
        mesh=mesh,
        in_specs=(P(("aux", "blk"), None, None), P("aux", None), P(), P("aux", None)),
        out_specs=P("blk", "aux", None),
        check_vma=False,
    )
```

profile of v0, /device:TPU:0, one launch (start us, length us, event | category | flops | bytes accessed | tf_op | source)
XLA Modules:
  0.0 535.0 jit_solution(6103885854642759354)
XLA Ops:
  6.5 24.0 %copy.18 = bf16[64,64,1024]{1,0,2:T(8,128)(2,1)} copy(bf16[64,64,1024]{2,1,0:T(8,128)(2,1)} %param.4) | data formatting | bytes 16777216 | tf_op args[0]
  30.5 16.9 %reshape.23 = bf16[8,2,262144]{2,1,0:T(2,128)(2,1)} reshape(bf16[1024,64,64]{2,1,0:T(8,128)(2,1)} %bitcast.79) | data formatting | bytes 16777216
  47.4 6.5 %all-to-all-start = ((bf16[8,2,262144]{2,1,0:T(2,128)(2,1)}), bf16[8,2,262144]{2,1,0:T(2,128)(2,1)}, u32[]{:S(2)}, u32[]{:S(2)}) async-start(bf16[8,2,262144]{2,1,0:T(2,128)(2,1)} %reshape.23), calls=%async_computation | async-start | bytes 16777216 | tf_op jit(solution)/shard_map/all_to_all | solution.py:34
  54.2 183.7 %all-to-all-done = bf16[8,2,262144]{2,1,0:T(2,128)(2,1)} async-done(((bf16[8,2,262144]{2,1,0:T(2,128)(2,1)}), bf16[8,2,262144]{2,1,0:T(2,128)(2,1)}, u32[]{:S(2)}, u32[]{:S(2)}) %all-to-all-start) | async-done | bytes 8388640 | tf_op jit(solution)/shard_map/all_to_all | solution.py:34
  237.9 16.5 %reshape.24 = bf16[1024,64,64]{2,1,0:T(8,128)(2,1)} reshape(bf16[8,2,262144]{2,1,0:T(2,128)(2,1)} %all-to-all-done) | data formatting | bytes 16777216
  254.3 27.7 %copy.19 = bf16[64,64,8,128]{3,0,2,1:T(8,128)(2,1)} copy(bf16[64,64,8,128]{1,0,3,2:T(8,128)(2,1)} %bitcast.78) | data formatting | bytes 16777216 | tf_op jit(solution)/shard_map/all_to_all | solution.py:34
  282.1 8.1 %multiply_convert_fusion = bf16[512,64,128]{2,0,1:T(8,128)(2,1)S(1)} fusion(bf16[512,64,128]{2,0,1:T(8,128)(2,1)} %bitcast.80, f32[512]{0:T(512)S(1)} %broadcast_bitcast_fusion, bf16[512,512]{1,0:T(8,128)(2,1)S(1)} %copy-done), kind=kOutput, calls=%fused_computation | convolution fusion | flops 4303355904 | bytes 17303552 | tf_op jit(solution)/shard_map/pq,qjn->pjn/dot_general | solution.py:18
  290.2 1.3 collective-permute-start
  291.5 13.8 %collective-permute-done = bf16[512,64,128]{2,0,1:T(8,128)(2,1)S(1)} collective-permute-done((bf16[512,64,128]{2,0,1:T(8,128)(2,1)S(1)}, bf16[512,64,128]{2,0,1:T(8,128)(2,1)S(1)}, u32[]{:S(2)}, u32[]{:S(2)}) %collective-permute-start) | collective-permute-done | bytes 8388640 | tf_op jit(solution)/shard_map/ppermute | solution.py:14
  305.3 1.5 collective-permute-start.1
  308.9 2.5 fusion.4
  311.4 87.7 %collective-permute-done.1 = bf16[512,64,128]{2,0,1:T(8,128)(2,1)S(1)} collective-permute-done((bf16[512,64,128]{2,0,1:T(8,128)(2,1)S(1)}, bf16[512,64,128]{2,0,1:T(8,128)(2,1)S(1)}, u32[]{:S(2)}, u32[]{:S(2)}) %collective-permute-start.1) | collective-permute-done | bytes 8388640 | tf_op jit(solution)/shard_map/ppermute | solution.py:14
  399.1 2.4 fusion.3
  401.5 82.1 %collective-permute-start.2 = (bf16[2,128,128]{1,2,0:T(8,128)(2,1)S(1)}, bf16[2,128,128]{1,2,0:T(8,128)(2,1)S(1)}, u32[]{:S(2)}, u32[]{:S(2)}) collective-permute-start(bf16[2,128,128]{1,2,0:T(8,128)(2,1)S(1)} %pad_maximum_fusion), channel_id=1, source_target_pairs={{0,1},{1,2},{2,3},{3,4},{4,5},{5,6},{6,7},{8,9},{9,10},{10,11},{11... | collective-permute-start | bytes 196616 | tf_op jit(solution)/shard_map/ppermute | solution.py:14
  483.6 0.9 collective-permute-done.2
  484.5 2.3 collective-permute-start.3
  487.8 8.2 %fusion.2 = f32[5,128,128]{2,1,0:T(8,128)S(1)} fusion(f32[5,128,128]{2,1,0:T(8,128)S(1)} %constant_dynamic-update-slice_fusion, bf16[512,64,128]{2,0,1:T(8,128)(2,1)} %copy-done.1, f32[]{:T(128)} %bitcast.16), kind=kOutput, calls=%fused_computation.4 | convolution fusion | flops 1073758208 | bytes 16843264 | tf_op jit(solution)/shard_map/dot_general | solution.py:44
  496.0 0.7 copy-done.2
  496.8 27.1 %reduce-scatter.2.cloned.1.call-done = f32[5,32,128]{2,1,0:T(8,128)} async-done(((f32[5,128,128]{2,1,0:T(8,128)}), f32[5,32,128]{2,1,0:T(8,128)}) %reduce-scatter.2.cloned.1.call-update) | async-done | bytes 81936 | tf_op jit(solution)/shard_map/reduce_scatter | solution.py:65
  523.9 0.7 constant_dynamic-update-slice_fusion.6
  524.6 0.7 constant_dynamic-update-slice_fusion.5
  525.4 0.7 constant_dynamic-update-slice_fusion.4
  526.1 0.7 constant_dynamic-update-slice_fusion.3
  526.8 0.7 constant_dynamic-update-slice_fusion.2
  (32 shorter events, 2.0 us)
Async XLA Ops:
  6.5 275.5 %copy-start = (bf16[512,512]{1,0:T(8,128)(2,1)S(1)}, bf16[512,512]{1,0:T(8,128)(2,1)}, u32[]{:S(2)}) copy-start(bf16[512,512]{1,0:T(8,128)(2,1)} %param.5) | copy-start | bytes 1572868
  47.4 6.5 %copy-start.4 = (s32[4,8]{1,0:T(4,128)S(1)}, s32[4,8]{1,0:T(4,128)}, u32[]{:S(2)}) copy-start(s32[4,8]{1,0:T(4,128)} %param.7) | copy-start | bytes 388
  47.4 190.4 %all-to-all-start = ((bf16[8,2,262144]{2,1,0:T(2,128)(2,1)}), bf16[8,2,262144]{2,1,0:T(2,128)(2,1)}, u32[]{:S(2)}, u32[]{:S(2)}) async-start(bf16[8,2,262144]{2,1,0:T(2,128)(2,1)} %reshape.23), calls=%async_computation | async-start | bytes 16777216 | tf_op jit(solution)/shard_map/all_to_all | solution.py:34
  53.9 470.0 %reduce-scatter.2.cloned.1.call-start = ((), (), s32[]{:S(2)}) async-start(), calls=%async_computation.2 | async-start | bytes 409600 | tf_op jit(solution)/shard_map/reduce_scatter | solution.py:65
  282.1 24.7 %copy-start.5 = (s32[15,2]{0,1:T(2,128)S(1)}, s32[15,2]{0,1:T(2,128)}, u32[]{:S(2)}) copy-start(s32[15,2]{0,1:T(2,128)} %param.6) | copy-start | bytes 364
  290.2 108.9 %copy-start.1 = (bf16[512,64,128]{2,0,1:T(8,128)(2,1)}, bf16[512,64,128]{2,0,1:T(8,128)(2,1)S(1)}, u32[]{:S(2)}) copy-start(bf16[512,64,128]{2,0,1:T(8,128)(2,1)S(1)} %multiply_convert_fusion) | copy-start | bytes 25165828
  290.2 15.1 %collective-permute-start = (bf16[512,64,128]{2,0,1:T(8,128)(2,1)S(1)}, bf16[512,64,128]{2,0,1:T(8,128)(2,1)S(1)}, u32[]{:S(2)}, u32[]{:S(2)}) collective-permute-start(bf16[512,64,128]{2,0,1:T(8,128)(2,1)S(1)} %multiply_convert_fusion), channel_id=1, source_target_pairs={{1,0},{2,1},{3,2},{4,3},{5,4},{6,5},{7,6},{9,8},{10,9},{11,10},{12... | collective-permute-start | bytes 25165832 | tf_op jit(solution)/shard_map/ppermute | solution.py:14
  305.3 93.8 %collective-permute-start.1 = (bf16[512,64,128]{2,0,1:T(8,128)(2,1)S(1)}, bf16[512,64,128]{2,0,1:T(8,128)(2,1)S(1)}, u32[]{:S(2)}, u32[]{:S(2)}) collective-permute-start(bf16[512,64,128]{2,0,1:T(8,128)(2,1)S(1)} %collective-permute-done), channel_id=1, source_target_pairs={{1,0},{2,1},{3,2},{4,3},{5,4},{6,5},{7,6},{9,8},{10,9},{11,10},{12... | collective-permute-start | bytes 25165832 | tf_op jit(solution)/shard_map/ppermute | solution.py:14
  401.5 83.0 %collective-permute-start.2 = (bf16[2,128,128]{1,2,0:T(8,128)(2,1)S(1)}, bf16[2,128,128]{1,2,0:T(8,128)(2,1)S(1)}, u32[]{:S(2)}, u32[]{:S(2)}) collective-permute-start(bf16[2,128,128]{1,2,0:T(8,128)(2,1)S(1)} %pad_maximum_fusion), channel_id=1, source_target_pairs={{0,1},{1,2},{2,3},{3,4},{4,5},{5,6},{6,7},{8,9},{9,10},{10,11},{11... | collective-permute-start | bytes 196616 | tf_op jit(solution)/shard_map/ppermute | solution.py:14
  484.5 3.2 collective-permute-start.3
  496.0 0.7 copy-start.2
  527.5 0.6 copy-start.3
Sparse Core Ops, SparseCore 0:
  496.9 26.9 reduce-scatter.1
where the time goes:
time: 537 us; the launch traced here: 535 us
  waiting for transfers between devices  313 us (58%)
  starting transfers between devices  93.7 us (17%)
  local copies, waits for them, and re-layouts  91 us (17%)
  matrix products  21.2 us (4%)
  between operations  15.5 us (3%)
    all_to_all x1, waiting for transfers between devices, local(): lax.all_to_all(integrals, 'blk', split_axis=2, concat_axis=0, tiled=True)  184 us
    ppermute x4, waiting for transfers between devices, from_behind(): return lax.ppermute(array, axis, pairs)  102 us
    ppermute x4, starting transfers between devices, from_behind(): return lax.ppermute(array, axis, pairs)  87.2 us
    unnamed x22, local copies, waits for them, and re-layouts  61.6 us
    all_to_all x1, local copies, waits for them, and re-layouts, local(): lax.all_to_all(integrals, 'blk', split_axis=2, concat_axis=0, tiled=True)  27.7 us
    reduce_scatter x1, waiting for transfers between devices, local(): lax.psum_scatter(whole_band, 'aux', scatter_dimension=1, tiled=True)  27.1 us
    dot_general x3, matrix products, make_tile(): lax.dot_general(flat_own, partner.reshape(-1, BS), (((0,), (0,)), ((), ()...  13.1 us
  transfers between devices with their start and end apart: 6, of which 6 were waited for; matrix products, arithmetic and copies ran while one was open for 1% of the time, Pallas kernels for 0%

commit v1 on v0

--- a/solution.py
+++ b/solution.py
@@ -6,6 +6,12 @@
 BS = 128
 QB = 128
 SPAN = 3
+
+
+def swap_blocks(x, axis, split, join):
+    parts = jnp.split(x, lax.axis_size(axis), axis=split)
+    received = lax.all_to_all(jnp.stack(parts), axis, 0, 0)
+    return jnp.concatenate(received, axis=join)
 
 
 def from_behind(array, axis, by):
@@ -30,9 +36,7 @@
     one_hot = (block_ids == position).astype(jnp.int32)
     column = jnp.sum(aux_mask * one_hot[None, :], axis=1)
     own_mask = jnp.repeat(column, QB).astype(jnp.float32)
-    own_block = fit_block(
-        metric, lax.all_to_all(integrals, "blk", split_axis=2, concat_axis=0, tiled=True), own_mask
-    )
+    own_block = fit_block(metric, swap_blocks(integrals, "blk", 2, 0), own_mask)
     partners = [own_block]
     current = own_block
     for turn_index in range(SPAN - 1):

time: 537 us -> 503 us (0.937)
  local copies, waits for them, and re-layouts: 91 us -> 24.3 us
  matrix products: 21.2 us -> 57.2 us
    unnamed x22 -> x26, local copies, waits for them, and re-layouts: 61.6 us -> 20.4 us
    dot_general x1, matrix products: 8.13 us -> 37.7 us  [fit_block(): jnp.einsum('pq,qjn->pjn', metric, slab_piece, preferred_element_type=jnp....]
    all_to_all x1 -> x0, local copies, waits for them, and re-layouts: 27.7 us -> none  [local(): lax.all_to_all(integrals, 'blk', split_axis=2, concat_axis=0, tiled=True)]
    dot_general x3, matrix products: 13.1 us -> 19.5 us  [make_tile(): lax.dot_general(flat_own, partner.reshape(-1, BS), (((0,), (0,)), ((), ()...]
where the time goes in v1:
time: 503 us; the launch traced here: 502 us
  waiting for transfers between devices  311 us (62%)
  starting transfers between devices  93.5 us (19%)
  matrix products  57.2 us (11%)
  local copies, waits for them, and re-layouts  24.3 us (5%)
  between operations  15.6 us (3%)
    all_to_all x1, waiting for transfers between devices, swap_blocks(): received = lax.all_to_all(jnp.stack(parts), axis, 0, 0)  184 us
    ppermute x4, waiting for transfers between devices, from_behind(): return lax.ppermute(array, axis, pairs)  99.8 us
    ppermute x4, starting transfers between devices, from_behind(): return lax.ppermute(array, axis, pairs)  87 us
    dot_general x1, matrix products, fit_block(): jnp.einsum('pq,qjn->pjn', metric, slab_piece, preferred_element_type=jnp....  37.7 us
    reduce_scatter x1, waiting for transfers between devices, local(): lax.psum_scatter(whole_band, 'aux', scatter_dimension=1, tiled=True)  27.2 us
    unnamed x26, local copies, waits for them, and re-layouts  20.4 us
    dot_general x3, matrix products, make_tile(): lax.dot_general(flat_own, partner.reshape(-1, BS), (((0,), (0,)), ((), ()...  19.5 us
  transfers between devices with their start and end apart: 6, of which 6 were waited for; matrix products, arithmetic and copies ran while one was open for 1% of the time, Pallas kernels for 0%

profile of v1, /device:TPU:0, one launch (start us, length us, event | category | flops | bytes accessed | tf_op | source)
XLA Modules:
  0.0 501.5 jit_solution(6617565357518721746)
XLA Ops:
  6.5 2.4 bitcast_dynamic-update-slice_fusion.7
  8.9 2.2 bitcast_dynamic-update-slice_fusion.6
  11.2 2.3 bitcast_dynamic-update-slice_fusion.5
  13.5 2.3 bitcast_dynamic-update-slice_fusion.4
  15.8 2.3 bitcast_dynamic-update-slice_fusion.3
  18.1 2.3 bitcast_dynamic-update-slice_fusion.2
  20.4 2.3 bitcast_dynamic-update-slice_fusion.1
  22.6 2.3 bitcast_dynamic-update-slice_fusion
  24.9 6.5 %all-to-all-start = ((bf16[8,64,64,128]{3,2,1,0:T(8,128)(2,1)}), bf16[8,64,64,128]{3,2,1,0:T(8,128)(2,1)}, u32[]{:S(2)}, u32[]{:S(2)}) async-start(bf16[8,64,64,128]{3,2,1,0:T(8,128)(2,1)} %bitcast_dynamic-update-slice_fusion), calls=%async_computation | async-start | bytes 16777216 | tf_op jit(solution)/shard_map/all_to_all | solution.py:13
  31.7 183.7 %all-to-all-done = bf16[8,64,64,128]{3,2,1,0:T(8,128)(2,1)} async-done(((bf16[8,64,64,128]{3,2,1,0:T(8,128)(2,1)}), bf16[8,64,64,128]{3,2,1,0:T(8,128)(2,1)}, u32[]{:S(2)}, u32[]{:S(2)}) %all-to-all-start) | async-done | bytes 8388640 | tf_op jit(solution)/shard_map/all_to_all | solution.py:13
  215.4 37.7 %fusion.1 = bf16[512,64,128]{0,2,1:T(8,128)(2,1)S(1)} fusion(f32[512]{0:T(512)S(1)} %broadcast_bitcast_fusion, bf16[512,64,128]{2,1,0:T(8,128)(2,1)} %bitcast.8, bf16[512,512]{1,0:T(8,128)(2,1)S(1)} %copy-done), kind=kOutput, calls=%fused_computation.2 | convolution fusion | flops 4303355904 | bytes 17303552 | tf_op jit(solution)/shard_map/pq,qjn->pjn/dot_general | solution.py:24
  253.1 1.3 collective-permute-start
  254.4 13.9 %collective-permute-done = bf16[512,64,128]{0,2,1:T(8,128)(2,1)} collective-permute-done((bf16[512,64,128]{0,2,1:T(8,128)(2,1)S(1)}, bf16[512,64,128]{0,2,1:T(8,128)(2,1)}, u32[]{:S(2)}, u32[]{:S(2)}) %collective-permute-start) | collective-permute-done | bytes 8388640 | tf_op jit(solution)/shard_map/ppermute | solution.py:20
  268.3 1.3 collective-permute-start.1
  271.7 5.7 %fusion.8 = f32[128,128]{1,0:T(8,128)S(1)} fusion(bf16[512,64,128]{0,2,1:T(8,128)(2,1)S(1)} %fusion.1, bf16[512,64,128]{0,2,1:T(8,128)(2,1)} %collective-permute-done, f32[]{:T(128)} %bitcast.15), kind=kOutput, calls=%fused_computation.10 | convolution fusion | flops 1073758208 | bytes 16842756 | tf_op jit(solution)/shard_map/dot_general | solution.py:48
  277.4 85.0 %collective-permute-done.1 = bf16[512,64,128]{0,2,1:T(8,128)(2,1)} collective-permute-done((bf16[512,64,128]{0,2,1:T(8,128)(2,1)}, bf16[512,64,128]{0,2,1:T(8,128)(2,1)}, u32[]{:S(2)}, u32[]{:S(2)}) %collective-permute-start.1) | collective-permute-done | bytes 8388640 | tf_op jit(solution)/shard_map/ppermute | solution.py:20
  362.4 5.7 %fusion.7 = f32[128,128]{1,0:T(8,128)S(1)} fusion(bf16[512,64,128]{0,2,1:T(8,128)(2,1)S(1)} %fusion.1, bf16[512,64,128]{0,2,1:T(8,128)(2,1)} %collective-permute-done.1, f32[]{:T(128)} %bitcast.19), kind=kOutput, calls=%fused_computation.8 | convolution fusion | flops 1073758208 | bytes 16842756 | tf_op jit(solution)/shard_map/dot_general | solution.py:48
  368.1 82.1 %collective-permute-start.2 = (bf16[2,128,128]{1,2,0:T(8,128)(2,1)S(1)}, bf16[2,128,128]{1,2,0:T(8,128)(2,1)S(1)}, u32[]{:S(2)}, u32[]{:S(2)}) collective-permute-start(bf16[2,128,128]{1,2,0:T(8,128)(2,1)S(1)} %pad_maximum_fusion), channel_id=1, source_target_pairs={{0,1},{1,2},{2,3},{3,4},{4,5},{5,6},{6,7},{8,9},{9,10},{10,11},{11... | collective-permute-start | bytes 196616 | tf_op jit(solution)/shard_map/ppermute | solution.py:20
  450.2 0.9 collective-permute-done.2
  451.1 2.3 collective-permute-start.3
  454.4 8.1 %fusion.6 = f32[5,128,128]{2,1,0:T(8,128)S(1)} fusion(f32[5,128,128]{2,1,0:T(8,128)S(1)} %constant_dynamic-update-slice_fusion, bf16[512,64,128]{0,2,1:T(8,128)(2,1)} %copy-done.1, f32[]{:T(128)} %bitcast.23), kind=kOutput, calls=%fused_computation.6 | convolution fusion | flops 1073758208 | bytes 16843264 | tf_op jit(solution)/shard_map/dot_general | solution.py:48
  463.3 27.2 %reduce-scatter.2.cloned.1.call-done = f32[5,32,128]{2,1,0:T(8,128)} async-done(((f32[5,128,128]{2,1,0:T(8,128)}), f32[5,32,128]{2,1,0:T(8,128)}) %reduce-scatter.2.cloned.1.call-update) | async-done | bytes 81936 | tf_op jit(solution)/shard_map/reduce_scatter | solution.py:69
  490.5 0.7 constant_dynamic-update-slice_fusion.6
  492.6 0.7 constant_dynamic-update-slice_fusion.3
  (36 shorter events, 4.9 us)
Async XLA Ops:
  6.5 208.8 %copy-start = (bf16[512,512]{1,0:T(8,128)(2,1)S(1)}, bf16[512,512]{1,0:T(8,128)(2,1)}, u32[]{:S(2)}) copy-start(bf16[512,512]{1,0:T(8,128)(2,1)} %param.5) | copy-start | bytes 1572868
  24.9 6.5 %copy-start.4 = (s32[4,8]{1,0:T(4,128)S(1)}, s32[4,8]{1,0:T(4,128)}, u32[]{:S(2)}) copy-start(s32[4,8]{1,0:T(4,128)} %param.7) | copy-start | bytes 388
  24.9 190.4 %all-to-all-start = ((bf16[8,64,64,128]{3,2,1,0:T(8,128)(2,1)}), bf16[8,64,64,128]{3,2,1,0:T(8,128)(2,1)}, u32[]{:S(2)}, u32[]{:S(2)}) async-start(bf16[8,64,64,128]{3,2,1,0:T(8,128)(2,1)} %bitcast_dynamic-update-slice_fusion), calls=%async_computation | async-start | bytes 16777216 | tf_op jit(solution)/shard_map/all_to_all | solution.py:13
  31.4 459.1 %reduce-scatter.2.cloned.1.call-start = ((), (), s32[]{:S(2)}) async-start(), calls=%async_computation.2 | async-start | bytes 409600 | tf_op jit(solution)/shard_map/reduce_scatter | solution.py:69
  215.4 54.2 %copy-start.5 = (s32[15,2]{0,1:T(2,128)S(1)}, s32[15,2]{0,1:T(2,128)}, u32[]{:S(2)}) copy-start(s32[15,2]{0,1:T(2,128)} %param.6) | copy-start | bytes 364
  253.1 109.3 %copy-start.1 = (bf16[512,64,128]{0,2,1:T(8,128)(2,1)}, bf16[512,64,128]{0,2,1:T(8,128)(2,1)S(1)}, u32[]{:S(2)}) copy-start(bf16[512,64,128]{0,2,1:T(8,128)(2,1)S(1)} %fusion.1) | copy-start | bytes 25165828
  253.1 15.2 %collective-permute-start = (bf16[512,64,128]{0,2,1:T(8,128)(2,1)S(1)}, bf16[512,64,128]{0,2,1:T(8,128)(2,1)}, u32[]{:S(2)}, u32[]{:S(2)}) collective-permute-start(bf16[512,64,128]{0,2,1:T(8,128)(2,1)S(1)} %fusion.1), channel_id=1, source_target_pairs={{1,0},{2,1},{3,2},{4,3},{5,4},{6,5},{7,6},{9,8},{10,9},{11,10},{12... | collective-permute-start | bytes 25165832 | tf_op jit(solution)/shard_map/ppermute | solution.py:20
  268.3 94.1 %collective-permute-start.1 = (bf16[512,64,128]{0,2,1:T(8,128)(2,1)}, bf16[512,64,128]{0,2,1:T(8,128)(2,1)}, u32[]{:S(2)}, u32[]{:S(2)}) collective-permute-start(bf16[512,64,128]{0,2,1:T(8,128)(2,1)} %collective-permute-done), channel_id=1, source_target_pairs={{1,0},{2,1},{3,2},{4,3},{5,4},{6,5},{7,6},{9,8},{10,9},{11,10},{12... | collective-permute-start | bytes 25165832 | tf_op jit(solution)/shard_map/ppermute | solution.py:20
  368.1 83.0 %collective-permute-start.2 = (bf16[2,128,128]{1,2,0:T(8,128)(2,1)S(1)}, bf16[2,128,128]{1,2,0:T(8,128)(2,1)S(1)}, u32[]{:S(2)}, u32[]{:S(2)}) collective-permute-start(bf16[2,128,128]{1,2,0:T(8,128)(2,1)S(1)} %pad_maximum_fusion), channel_id=1, source_target_pairs={{0,1},{1,2},{2,3},{3,4},{4,5},{5,6},{6,7},{8,9},{9,10},{10,11},{11... | collective-permute-start | bytes 196616 | tf_op jit(solution)/shard_map/ppermute | solution.py:20
  451.1 3.2 collective-permute-start.3
  462.6 0.7 copy-start.2
  494.1 0.6 copy-start.3
Sparse Core Ops, SparseCore 0:
  463.4 27.0 reduce-scatter.1
